TPU v7x, 32 devices: a whole 2x2x4 slice. The times are simulated.
32 devices in a mesh: row: 8 (over y, x, core), col: 4 (over z).
Axes of the slice: x: 2, y: 2, z: 4, core: 2. Of those that a mesh axis runs over, the one named last changes fastest.
Arguments:
- features: bfloat16 [16384, 512], P(('row', 'col')), may hold values from -6 to 6
- weight: bfloat16 [512, 512], replicated, may hold values from -0.25 to 0.25
- bias: float32 [512], replicated, may hold values from -3 to 3
- cotangent: bfloat16 [16384, 512], P(('row', 'col')), may hold values from -6 to 6
- tile_values: bfloat16 [8, 4, 64, 128, 128], P('row', 'col'), may hold values from -0.1875 to 0.1875
- tile_rows: int32 [8, 4, 64], P('row', 'col'), may hold values from 0 to 127, as said below
- tile_cols: int32 [8, 4, 64], P('row', 'col'), may hold values from 0 to 127, as said below
- tile_counts: int32 [8, 4], P('row', 'col'), may hold values from 1 to 64
Outputs:
- output: bfloat16 [16384, 512], P(('row', 'col'))
- feature_grad: bfloat16 [16384, 512], P(('row', 'col'))
- weight_grad: float32 [512, 512], replicated
- bias_grad: float32 [512], replicated
Inputs may be any that keep to these rules, and one draw needn't show every extreme that they name: `tile_rows`: A tile on device (p, q) has its row block in row group p, that is row block // 16 == p, and its column block's atoms on devices of index q along col, that is (column block // 4) % 4 == q. The rows of features held by device (p, q) are blocks p * 4 * 4 + q * 4 to that plus 4 - 1. Row and column pairs may repeat. `tile_cols`: among one device's live tiles at most 16 have their row block held by any one device of that row group, and at most 8 have their column block held by any one device of that column group.
All inputs are finite; a program needn't handle non-finite values.
Results may differ from a plain program's by a relative error of at most 0.013.
Values may be sent and summed in bfloat16 or wider, within the bound.
A program may use at most 128 MiB of HBM per device.

v0:
```python
import math
import jax
import jax.numpy as jnp
from jax import lax
from jax.sharding import PartitionSpec as P


def sum_rows(products, local_ids, alive_mask, total_blocks):
    block_size = products.shape[1]
    feature_width = products.shape[2]
    target_ids = jnp.where(alive_mask, local_ids, total_blocks)
    blank_sum = jnp.zeros((total_blocks, block_size, feature_width), jnp.float32)
    summed = blank_sum.at[target_ids].add(products, mode="drop")
    return summed.reshape(total_blocks * block_size, feature_width)


def on_device(features, weight, bias, cotangent, tile_values, tile_rows, tile_cols, tile_counts):
    row_count = lax.axis_size("row")
    col_count = lax.axis_size("col")
    node_dev, feature_width = features.shape
    slot_count = tile_values.shape[2]
    block_size = tile_values.shape[3]
    blk_dev = node_dev // block_size
    atom_count = node_dev * row_count * col_count
    values = tile_values.reshape(slot_count, block_size, block_size)
    alive_mask = jnp.arange(slot_count) < tile_counts.reshape(())
    row_local = tile_rows.reshape(slot_count) % (blk_dev * col_count)
    col_ids = tile_cols.reshape(slot_count)
    col_local = col_ids // (blk_dev * col_count) * blk_dev + col_ids % blk_dev
    gathered = lax.all_gather(features, "row", axis=0, tiled=True).reshape(
        row_count * blk_dev, block_size, feature_width
    )
    sources = gathered[col_local]
    products = jnp.einsum("kab,kbd->kad", values, sources, preferred_element_type=jnp.float32)
    partial_value = sum_rows(products, row_local, alive_mask, blk_dev * col_count)
    summed = lax.psum_scatter(partial_value, "col", scatter_dimension=0, tiled=True)
    aggregated = summed.astype(jnp.bfloat16)
    pre_act = jnp.dot(aggregated, weight, preferred_element_type=jnp.float32) + bias
    sigm = jax.nn.sigmoid(pre_act)
    output = (pre_act * sigm).astype(jnp.bfloat16)
    grad_pre = (cotangent.astype(jnp.float32) * sigm * (1.0 + pre_act * (1.0 - sigm))).astype(
        jnp.bfloat16
    )
    scale = 1.0 / math.sqrt(atom_count)
    weight_part = jnp.dot(aggregated.T, grad_pre, preferred_element_type=jnp.float32) * scale
    bias_part = jnp.sum(grad_pre.astype(jnp.float32), axis=0) * scale
    weight_grad, bias_grad = lax.psum((weight_part, bias_part), ("row", "col"))
    grad_agg = jnp.dot(grad_pre, weight.T, preferred_element_type=jnp.float32).astype(jnp.bfloat16)
    spread = lax.all_gather(grad_agg, "col", axis=0, tiled=True).reshape(
        col_count * blk_dev, block_size, feature_width
    )
    upstream = spread[row_local]
    back_products = jnp.einsum("kba,kbd->kad", values, upstream, preferred_element_type=jnp.float32)
    grad_partial = sum_rows(back_products, col_local, alive_mask, blk_dev * row_count)
    grad_summed = lax.psum_scatter(
        grad_partial.astype(jnp.bfloat16), "row", scatter_dimension=0, tiled=True
    )
    return (output, grad_summed, weight_grad, bias_grad)


def solution(mesh):
    return jax.shard_map(
        on_device,
        mesh=mesh,
        in_specs=(
            P(("row", "col"), None),
            P(),
            P(),
            P(("row", "col"), None),
            P("row", "col", None, None, None),
            P("row", "col", None),
            P("row", "col", None),
            P("row", "col"),
        ),
        out_specs=(P(("row", "col"), None), P(("row", "col"), None), P(), P()),
        check_vma=False,
    )
```

profile of v0, /device:TPU:0, one launch (start us, length us, event | category | flops | bytes accessed | tf_op | source)
XLA Modules:
  0.0 449.0 jit_solution(17194235437523508426)
XLA Ops:
  7.2 0.0 copy-start
  7.2 0.0 all-gather.3.cloned.1.call-start
  7.2 0.7 all-gather.3.cloned.1.call-update
  7.9 0.0 reduce-scatter.3.cloned.1.call-start
  8.6 0.7 fusion.8
  9.3 0.7 fusion.9
  10.0 39.2 %all-gather.3.cloned.1.call-done = bf16[4096,512]{1,0:T(8,128)(2,1)} async-done(((bf16[512,512]{1,0:T(8,128)(2,1)}), bf16[4096,512]{1,0:T(8,128)(2,1)}) %all-gather.3.cloned.1.call-update) | async-done | bytes 4194320 | tf_op jit(solution)/shard_map/all_gather | solution.py:30
  49.2 7.7 %gather_fusion = bf16[64,128,512]{2,1,0:T(8,128)(2,1)} fusion(bf16[32,128,512]{2,1,0:T(8,128)(2,1)} %bitcast.47, s32[1024]{0:T(1024)S(1)} %pad_clamp_fusion.1), kind=kCustom, calls=%fused_computation | custom fusion | bytes 16777472 | tf_op jit(solution)/shard_map/gather | solution.py:33
  56.9 0.0 copy-done
  56.9 11.5 %convolution_bitcast_fusion.1 = f32[64,128,512]{1,2,0:T(8,128)} fusion(bf16[64,128,512]{2,1,0:T(8,128)(2,1)} %gather_fusion, bf16[1,1,64,128,128]{4,3,2,1,0:T(8,128)(2,1)S(1)} %copy-done), kind=kOutput, calls=%fused_computation.5 | convolution fusion | flops 1073741824 | bytes 27262976 | tf_op jit(solution)/shard_map/kab,kbd->kad/dot_general | solution.py:34
  68.4 17.5 %copy.15 = f32[64,128,512]{2,1,0:T(8,128)} copy(f32[64,128,512]{1,2,0:T(8,128)} %convolution_bitcast_fusion.1) | data formatting | bytes 33554432 | tf_op jit(solution)/shard_map/kab,kbd->kad/dot_general | solution.py:34
  85.9 2.5 broadcast_in_dim.7
  88.4 0.0 copy-start.1
  88.4 0.0 copy-start.2
  88.4 34.5 %scatter_fusion = f32[16,128,512]{2,1,0:T(8,128)} fusion(f32[16,128,512]{2,1,0:T(8,128)} %broadcast_in_dim.7, s32[64]{0:T(128)S(1)} %fusion.6, f32[64,128,512]{2,1,0:T(8,128)} %copy.15), kind=kCustom, calls=%fused_computation.2 | custom fusion | flops 4194304 | bytes 50331904 | tf_op jit(solution)/shard_map/scatter-add | solution.py:13
  122.8 0.0 reduce-scatter.3.cloned.1.call-update
  122.8 0.0 all-gather.5.cloned.1.call-start
  122.9 77.6 %reduce-scatter.3.cloned.1.call-done = f32[512,512]{1,0:T(8,128)} async-done(((f32[2048,512]{1,0:T(8,128)}), f32[512,512]{1,0:T(8,128)}) %reduce-scatter.3.cloned.1.call-update) | async-done | bytes 1048592 | tf_op jit(solution)/shard_map/reduce_scatter | solution.py:36
  200.5 0.0 copy-done.1
  200.5 0.0 copy-done.2
  200.5 3.0 convert_reduce_fusion
  203.5 1.3 convolution_convert_fusion
  204.8 0.0 all-gather.5.cloned.1.call-update
  204.8 0.0 all-reduce.2.cloned.1.call-start
  204.9 2.7 convolution_multiply_fusion
  207.5 0.0 all-reduce.2.cloned.1.call-update
  207.6 0.2 reduce-scatter.5.cloned.1.call-start
  207.8 43.3 %all-gather.5.cloned.1.call-done = bf16[2048,512]{1,0:T(8,128)(2,1)} async-done(((bf16[512,512]{1,0:T(8,128)(2,1)}), bf16[2048,512]{1,0:T(8,128)(2,1)}) %all-gather.5.cloned.1.call-update) | async-done | bytes 2097168 | tf_op jit(solution)/shard_map/all_gather | solution.py:49
  251.1 7.1 %gather_fusion.1 = bf16[64,128,512]{2,1,0:T(8,128)(2,1)} fusion(bf16[16,128,512]{2,1,0:T(8,128)(2,1)} %bitcast.46, s32[1024]{0:T(1024)S(1)} %pad_clamp_fusion), kind=kCustom, calls=%fused_computation.1 | custom fusion | bytes 16777472 | tf_op jit(solution)/shard_map/gather | solution.py:52
  258.2 11.6 %convolution_bitcast_fusion = f32[64,128,512]{1,2,0:T(8,128)} fusion(bf16[64,128,512]{2,1,0:T(8,128)(2,1)} %gather_fusion.1, bf16[1,1,64,128,128]{4,3,2,1,0:T(8,128)(2,1)S(1)} %copy-done), kind=kOutput, calls=%fused_computation.4 | convolution fusion | flops 1073741824 | bytes 27262976 | tf_op jit(solution)/shard_map/kba,kbd->kad/dot_general | solution.py:53
  269.8 17.5 %copy.17 = f32[64,128,512]{2,1,0:T(8,128)} copy(f32[64,128,512]{1,2,0:T(8,128)} %convolution_bitcast_fusion) | data formatting | bytes 33554432 | tf_op jit(solution)/shard_map/kba,kbd->kad/dot_general | solution.py:53
  287.3 4.3 broadcast_in_dim.8
  291.6 34.7 %scatter_fusion.1 = f32[32,128,512]{2,1,0:T(8,128)} fusion(f32[32,128,512]{2,1,0:T(8,128)} %broadcast_in_dim.8, s32[64]{0:T(128)S(1)} %get-tuple-element.8, f32[64,128,512]{2,1,0:T(8,128)} %copy.17), kind=kCustom, calls=%fused_computation.3 | custom fusion | flops 4194304 | bytes 50331904 | tf_op jit(solution)/shard_map/scatter-add | solution.py:13
  326.3 5.9 %convert_element_type.29 = bf16[32,128,512]{2,1,0:T(8,128)(2,1)} convert(f32[32,128,512]{2,1,0:T(8,128)} %scatter_fusion.1) | non-fusion elementwise | flops 2097152 | bytes 12582912 | tf_op jit(solution)/shard_map/convert_element_type | solution.py:56
  332.3 0.0 reduce-scatter.5.cloned.1.call-update
  332.3 39.5 %psum.15 = f32[512]{0:T(512)} all-reduce(f32[512]{0:T(512)S(1)} %broadcast_multiply_fusion), channel_id=1, replica_groups=mesh['row'=8,'col'=4] {'row','col'}, use_global_device_ids=true, to_apply=%region_6.7 | all-reduce | flops 512 | bytes 4096 | tf_op jit(solution)/shard_map/psum | solution.py:47
  371.8 14.5 %all-reduce.2.cloned.1.call-done = f32[512,512]{1,0:T(8,128)} async-done(((f32[512,512]{1,0:T(8,128)}), f32[512,512]{1,0:T(8,128)}) %all-reduce.2.cloned.1.call-update) | async-done | bytes 1048592 | tf_op jit(solution)/shard_map/psum | solution.py:47
  386.3 53.9 %reduce-scatter.5.cloned.1.call-done = bf16[512,512]{1,0:T(8,128)(2,1)} async-done(((bf16[4096,512]{1,0:T(8,128)(2,1)}), bf16[512,512]{1,0:T(8,128)(2,1)}) %reduce-scatter.5.cloned.1.call-update) | async-done | bytes 524304 | tf_op jit(solution)/shard_map/reduce_scatter | solution.py:55
  440.2 2.3 copy.24
  (5 shorter events, 0.0 us)
Async XLA Ops:
  7.2 49.8 %copy-start = (bf16[1,1,64,128,128]{4,3,2,1,0:T(8,128)(2,1)S(1)}, bf16[1,1,64,128,128]{4,3,2,1,0:T(8,128)(2,1)}, u32[]{:S(2)}) copy-start(bf16[1,1,64,128,128]{4,3,2,1,0:T(8,128)(2,1)} %param.12) | copy-start | bytes 6291460
  7.2 42.0 %all-gather.3.cloned.1.call-start = ((), (), s32[]{:S(2)}) async-start(), calls=%async_computation.2 | async-start | bytes 4718592 | tf_op jit(solution)/shard_map/all_gather | solution.py:30
  7.9 192.6 %reduce-scatter.3.cloned.1.call-start = ((), (), s32[]{:S(2)}) async-start(), calls=%async_computation.3 | async-start | bytes 5242880 | tf_op jit(solution)/shard_map/reduce_scatter | solution.py:36
  88.4 112.2 %copy-start.1 = (bf16[512,512]{1,0:T(8,128)(2,1)S(1)}, bf16[512,512]{1,0:T(8,128)(2,1)}, u32[]{:S(2)}) copy-start(bf16[512,512]{1,0:T(8,128)(2,1)} %param.9) | copy-start | bytes 1572868
  88.4 112.2 %copy-start.2 = (f32[512]{0:T(512)S(1)}, f32[512]{0:T(512)}, u32[]{:S(2)}) copy-start(f32[512]{0:T(512)} %param.10) | copy-start | bytes 6148
  122.8 128.3 %all-gather.5.cloned.1.call-start = ((), (), s32[]{:S(2)}) async-start(), calls=%async_computation.4 | async-start | bytes 2621440 | tf_op jit(solution)/shard_map/all_gather | solution.py:49
  204.8 181.5 %all-reduce.2.cloned.1.call-start = ((), (), s32[]{:S(2)}) async-start(), calls=%async_computation.6 | async-start | bytes 2097152 | tf_op jit(solution)/shard_map/psum | solution.py:47
  207.6 232.7 %reduce-scatter.5.cloned.1.call-start = ((), (), s32[]{:S(2)}) async-start(), calls=%async_computation.5 | async-start | bytes 4718592 | tf_op jit(solution)/shard_map/reduce_scatter | solution.py:55
Sparse Core Ops, SparseCore 0:
  9.9 39.2 all-gather.2
  123.0 77.4 reduce-scatter.2
  204.9 46.1 all-gather.4
  256.7 129.5 all-reduce.1
  390.1 50.0 reduce-scatter.4
where the time goes:
time: 450 us; the launch traced here: 449 us
  waiting for transfers between devices  229 us (51%)
  other arithmetic  76.5 us (17%)
  local copies, waits for them, and re-layouts  58.8 us (13%)
  blocking collectives  39.5 us (9%)
  matrix products  30 us (7%)
  between operations  14.5 us (3%)
    reduce_scatter x1, waiting for transfers between devices, on_device(): lax.psum_scatter(partial_value, 'col', scatter_dimension=0, tiled=True)  77.6 us
    scatter-add x2, other arithmetic, sum_rows(): summed = blank_sum.at[target_ids].add(products, mode='drop')  69.2 us
    reduce_scatter x1, waiting for transfers between devices, on_device(): lax.psum_scatter(grad_partial.astype(jnp.bfloat16), 'row', scatter_dimens...  53.9 us
    all_gather x1, waiting for transfers between devices, on_device(): lax.all_gather(grad_agg, 'col', axis=0, tiled=True)  43.3 us
    psum x1, blocking collectives, on_device(): weight_grad, bias_grad = lax.psum((weight_part, bias_part), ('row', 'col'))  39.5 us
    all_gather x1, waiting for transfers between devices, on_device(): lax.all_gather(features, 'row', axis=0, tiled=True)  39.2 us
    dot_general x1, local copies, waits for them, and re-layouts, on_device(): jnp.einsum('kba,kbd->kad', values, upstream, preferred_element_type=jnp.f...  17.5 us
    dot_general x1, local copies, waits for them, and re-layouts, on_device(): jnp.einsum('kab,kbd->kad', values, sources, preferred_element_type=jnp.fl...  17.5 us
  transfers between devices with their start and end apart: 5, of which 5 were waited for; matrix products, arithmetic and copies ran while one was open for 19% of the time, Pallas kernels for 0%

commit v1 on v0

--- a/solution.py
+++ b/solution.py
@@ -3,6 +3,23 @@
 import jax.numpy as jnp
 from jax import lax
 from jax.sharding import PartitionSpec as P
+
+
+def laid_out(tiles, dim):
+    shape = list(tiles.shape[1:])
+    shape[dim] *= tiles.shape[0]
+    return jnp.moveaxis(tiles, 0, dim).reshape(shape)
+
+
+def ring_gather(x, axis, dim):
+    size = lax.axis_size(axis)
+    right = [(i, (i + 1) % size) for i in range(size)]
+    pieces = [x]
+    while len(pieces) < size:
+        pieces.append(lax.ppermute(pieces[-1], axis, right))
+    index = lax.axis_index(axis)
+    pieces = jnp.stack(pieces)[(index - jnp.arange(size)) % size]
+    return laid_out(pieces, dim)
 
 
 def sum_rows(products, local_ids, alive_mask, total_blocks):
@@ -46,9 +63,7 @@
     bias_part = jnp.sum(grad_pre.astype(jnp.float32), axis=0) * scale
     weight_grad, bias_grad = lax.psum((weight_part, bias_part), ("row", "col"))
     grad_agg = jnp.dot(grad_pre, weight.T, preferred_element_type=jnp.float32).astype(jnp.bfloat16)
-    spread = lax.all_gather(grad_agg, "col", axis=0, tiled=True).reshape(
-        col_count * blk_dev, block_size, feature_width
-    )
+    spread = ring_gather(grad_agg, "col", 0).reshape(col_count * blk_dev, block_size, feature_width)
     upstream = spread[row_local]
     back_products = jnp.einsum("kba,kbd->kad", values, upstream, preferred_element_type=jnp.float32)
     grad_partial = sum_rows(back_products, col_local, alive_mask, blk_dev * row_count)

time: 450 us -> 434 us (0.964)
  waiting for transfers between devices: 229 us -> 208 us
    all_gather x1 -> x0, waiting for transfers between devices: 43.3 us -> none  [on_device(): lax.all_gather(grad_agg, 'col', axis=0, tiled=True)]
    ppermute x0 -> x3, waiting for transfers between devices: none -> 39.3 us  [ring_gather(): pieces.append(lax.ppermute(pieces[-1], axis, right))]
    psum x1, waiting for transfers between devices: 14.5 us -> 0.01 us  [on_device(): weight_grad, bias_grad = lax.psum((weight_part, bias_part), ('row', 'col'))]
  transfers between devices with their start and end apart: 5 -> 7, of which waited for: 5 -> 6; matrix products, arithmetic and copies ran while one was open for 19% -> 21% of each run, Pallas kernels for 0% -> 0%
where the time goes in v1:
time: 434 us; the launch traced here: 433 us
  waiting for transfers between devices  208 us (48%)
  other arithmetic  79.4 us (18%)
  local copies, waits for them, and re-layouts  62.5 us (14%)
  blocking collectives  37.1 us (9%)
  matrix products  30.2 us (7%)
  between operations  14.5 us (3%)
    reduce_scatter x1, waiting for transfers between devices, on_device(): lax.psum_scatter(partial_value, 'col', scatter_dimension=0, tiled=True)  77.6 us
    scatter-add x2, other arithmetic, sum_rows(): summed = blank_sum.at[target_ids].add(products, mode='drop')  69.1 us
    reduce_scatter x1, waiting for transfers between devices, on_device(): lax.psum_scatter(grad_partial.astype(jnp.bfloat16), 'row', scatter_dimens...  50.9 us
    ppermute x3, waiting for transfers between devices, ring_gather(): pieces.append(lax.ppermute(pieces[-1], axis, right))  39.3 us
    all_gather x1, waiting for transfers between devices, on_device(): lax.all_gather(features, 'row', axis=0, tiled=True)  39.2 us
    psum x1, blocking collectives, on_device(): weight_grad, bias_grad = lax.psum((weight_part, bias_part), ('row', 'col'))  37.1 us
    dot_general x1, local copies, waits for them, and re-layouts, on_device(): jnp.einsum('kba,kbd->kad', values, upstream, preferred_element_type=jnp.f...  17.5 us
    dot_general x1, local copies, waits for them, and re-layouts, on_device(): jnp.einsum('kab,kbd->kad', values, sources, preferred_element_type=jnp.fl...  17.5 us
  transfers between devices with their start and end apart: 7, of which 6 were waited for; matrix products, arithmetic and copies ran while one was open for 21% of the time, Pallas kernels for 0%

profile of v1, /device:TPU:0, one launch (start us, length us, event | category | flops | bytes accessed | tf_op | source)
XLA Modules:
  0.0 433.3 jit_solution(2334395772752603628)
XLA Ops:
  7.2 0.0 copy-start
  7.2 0.0 all-gather.2.cloned.1.call-start
  7.2 0.7 all-gather.2.cloned.1.call-update
  7.9 0.0 reduce-scatter.3.cloned.1.call-start
  8.6 0.7 fusion.9
  9.3 0.7 fusion.11
  10.0 39.2 %all-gather.2.cloned.1.call-done = bf16[4096,512]{1,0:T(8,128)(2,1)} async-done(((bf16[512,512]{1,0:T(8,128)(2,1)}), bf16[4096,512]{1,0:T(8,128)(2,1)}) %all-gather.2.cloned.1.call-update) | async-done | bytes 4194320 | tf_op jit(solution)/shard_map/all_gather | solution.py:47
  49.2 7.7 %gather_fusion = bf16[64,128,512]{2,1,0:T(8,128)(2,1)} fusion(bf16[32,128,512]{2,1,0:T(8,128)(2,1)} %bitcast.53, s32[1024]{0:T(1024)S(1)} %pad_clamp_fusion.2), kind=kCustom, calls=%fused_computation | custom fusion | bytes 16777472 | tf_op jit(solution)/shard_map/gather | solution.py:50
  56.9 0.0 copy-done
  56.9 11.5 %convolution_bitcast_fusion.1 = f32[64,128,512]{1,2,0:T(8,128)} fusion(bf16[64,128,512]{2,1,0:T(8,128)(2,1)} %gather_fusion, bf16[1,1,64,128,128]{4,3,2,1,0:T(8,128)(2,1)S(1)} %copy-done), kind=kOutput, calls=%fused_computation.6 | convolution fusion | flops 1073741824 | bytes 27262976 | tf_op jit(solution)/shard_map/kab,kbd->kad/dot_general | solution.py:51
  68.4 17.5 %copy.15 = f32[64,128,512]{2,1,0:T(8,128)} copy(f32[64,128,512]{1,2,0:T(8,128)} %convolution_bitcast_fusion.1) | data formatting | bytes 33554432 | tf_op jit(solution)/shard_map/kab,kbd->kad/dot_general | solution.py:51
  85.9 2.5 broadcast_in_dim.7
  88.4 0.0 copy-start.1
  88.4 0.0 copy-start.2
  88.4 34.5 %scatter_fusion = f32[16,128,512]{2,1,0:T(8,128)} fusion(f32[16,128,512]{2,1,0:T(8,128)} %broadcast_in_dim.7, s32[64]{0:T(128)S(1)} %fusion.7, f32[64,128,512]{2,1,0:T(8,128)} %copy.15), kind=kCustom, calls=%fused_computation.3 | custom fusion | flops 4194304 | bytes 50331904 | tf_op jit(solution)/shard_map/scatter-add | solution.py:30
  122.8 0.0 reduce-scatter.3.cloned.1.call-update
  122.8 0.0 all-reduce.2.cloned.1.call-start
  122.9 77.6 %reduce-scatter.3.cloned.1.call-done = f32[512,512]{1,0:T(8,128)} async-done(((f32[2048,512]{1,0:T(8,128)}), f32[512,512]{1,0:T(8,128)}) %reduce-scatter.3.cloned.1.call-update) | async-done | bytes 1048592 | tf_op jit(solution)/shard_map/reduce_scatter | solution.py:53
  200.5 0.0 copy-done.1
  200.5 0.0 copy-done.2
  200.5 3.0 convert_reduce_fusion
  203.5 1.5 convolution_convert_fusion
  205.0 1.5 collective-permute-start
  206.6 13.8 %collective-permute-done = bf16[512,512]{1,0:T(8,128)(2,1)} collective-permute-done((bf16[512,512]{1,0:T(8,128)(2,1)S(1)}, bf16[512,512]{1,0:T(8,128)(2,1)}, u32[]{:S(2)}, u32[]{:S(2)}) %collective-permute-start) | collective-permute-done | bytes 524320 | tf_op jit(solution)/shard_map/ppermute | solution.py:19
  220.3 0.0 collective-permute-start.1
  220.3 14.6 %collective-permute-done.1 = bf16[512,512]{1,0:T(8,128)(2,1)} collective-permute-done((bf16[512,512]{1,0:T(8,128)(2,1)}, bf16[512,512]{1,0:T(8,128)(2,1)}, u32[]{:S(2)}, u32[]{:S(2)}) %collective-permute-start.1) | collective-permute-done | bytes 524320 | tf_op jit(solution)/shard_map/ppermute | solution.py:19
  235.0 0.0 collective-permute-start.2
  235.0 2.7 convolution_multiply_fusion
  237.7 0.0 all-reduce.2.cloned.1.call-update
  237.7 0.2 reduce-scatter.5.cloned.1.call-start
  237.9 10.9 %collective-permute-done.2 = bf16[512,512]{1,0:T(8,128)(2,1)} collective-permute-done((bf16[512,512]{1,0:T(8,128)(2,1)}, bf16[512,512]{1,0:T(8,128)(2,1)}, u32[]{:S(2)}, u32[]{:S(2)}) %collective-permute-start.2) | collective-permute-done | bytes 524320 | tf_op jit(solution)/shard_map/ppermute | solution.py:19
  248.8 3.0 pad_maximum_fusion
  251.8 3.7 gather_fusion.1
  255.4 7.1 %gather_fusion.2 = bf16[64,128,512]{2,1,0:T(8,128)(2,1)} fusion(bf16[16,128,512]{2,1,0:T(8,128)(2,1)} %bitcast.52, s32[1024]{0:T(1024)S(1)} %pad_clamp_fusion), kind=kCustom, calls=%fused_computation.2 | custom fusion | bytes 16777472 | tf_op jit(solution)/shard_map/gather | solution.py:67
  262.6 11.5 %convolution_bitcast_fusion = f32[64,128,512]{1,2,0:T(8,128)} fusion(bf16[64,128,512]{2,1,0:T(8,128)(2,1)} %gather_fusion.2, bf16[1,1,64,128,128]{4,3,2,1,0:T(8,128)(2,1)S(1)} %copy-done), kind=kOutput, calls=%fused_computation.5 | convolution fusion | flops 1073741824 | bytes 27262976 | tf_op jit(solution)/shard_map/kba,kbd->kad/dot_general | solution.py:68
  274.1 17.5 %copy.17 = f32[64,128,512]{2,1,0:T(8,128)} copy(f32[64,128,512]{1,2,0:T(8,128)} %convolution_bitcast_fusion) | data formatting | bytes 33554432 | tf_op jit(solution)/shard_map/kba,kbd->kad/dot_general | solution.py:68
  291.6 4.3 broadcast_in_dim.8
  295.9 34.6 %scatter_fusion.1 = f32[32,128,512]{2,1,0:T(8,128)} fusion(f32[32,128,512]{2,1,0:T(8,128)} %broadcast_in_dim.8, s32[64]{0:T(128)S(1)} %get-tuple-element.8, f32[64,128,512]{2,1,0:T(8,128)} %copy.17), kind=kCustom, calls=%fused_computation.4 | custom fusion | flops 4194304 | bytes 50331904 | tf_op jit(solution)/shard_map/scatter-add | solution.py:30
  330.5 6.0 %convert_element_type.29 = bf16[32,128,512]{2,1,0:T(8,128)(2,1)} convert(f32[32,128,512]{2,1,0:T(8,128)} %scatter_fusion.1) | non-fusion elementwise | flops 2097152 | bytes 12582912 | tf_op jit(solution)/shard_map/convert_element_type | solution.py:71
  336.5 0.0 reduce-scatter.5.cloned.1.call-update
  336.5 37.1 %psum.15 = f32[512]{0:T(512)} all-reduce(f32[512]{0:T(512)S(1)} %broadcast_multiply_fusion), channel_id=1, replica_groups=mesh['row'=8,'col'=4] {'row','col'}, use_global_device_ids=true, to_apply=%region_6.7 | all-reduce | flops 512 | bytes 4096 | tf_op jit(solution)/shard_map/psum | solution.py:64
  373.6 0.0 all-reduce.2.cloned.1.call-done
  373.6 50.9 %reduce-scatter.5.cloned.1.call-done = bf16[512,512]{1,0:T(8,128)(2,1)} async-done(((bf16[4096,512]{1,0:T(8,128)(2,1)}), bf16[512,512]{1,0:T(8,128)(2,1)}) %reduce-scatter.5.cloned.1.call-update) | async-done | bytes 524304 | tf_op jit(solution)/shard_map/reduce_scatter | solution.py:70
  424.5 2.3 copy.24
  (7 shorter events, 0.0 us)
Async XLA Ops:
  7.2 49.8 %copy-start = (bf16[1,1,64,128,128]{4,3,2,1,0:T(8,128)(2,1)S(1)}, bf16[1,1,64,128,128]{4,3,2,1,0:T(8,128)(2,1)}, u32[]{:S(2)}) copy-start(bf16[1,1,64,128,128]{4,3,2,1,0:T(8,128)(2,1)} %param.12) | copy-start | bytes 6291460
  7.2 42.0 %all-gather.2.cloned.1.call-start = ((), (), s32[]{:S(2)}) async-start(), calls=%async_computation.2 | async-start | bytes 4718592 | tf_op jit(solution)/shard_map/all_gather | solution.py:47
  7.9 192.6 %reduce-scatter.3.cloned.1.call-start = ((), (), s32[]{:S(2)}) async-start(), calls=%async_computation.3 | async-start | bytes 5242880 | tf_op jit(solution)/shard_map/reduce_scatter | solution.py:53
  88.4 112.2 %copy-start.1 = (bf16[512,512]{1,0:T(8,128)(2,1)S(1)}, bf16[512,512]{1,0:T(8,128)(2,1)}, u32[]{:S(2)}) copy-start(bf16[512,512]{1,0:T(8,128)(2,1)} %param.9) | copy-start | bytes 1572868
  88.4 112.2 %copy-start.2 = (f32[512]{0:T(512)S(1)}, f32[512]{0:T(512)}, u32[]{:S(2)}) copy-start(f32[512]{0:T(512)} %param.10) | copy-start | bytes 6148
  122.8 250.8 %all-reduce.2.cloned.1.call-start = ((), (), s32[]{:S(2)}) async-start(), calls=%async_computation.5 | async-start | bytes 2097152 | tf_op jit(solution)/shard_map/psum | solution.py:64
  205.0 15.3 %collective-permute-start = (bf16[512,512]{1,0:T(8,128)(2,1)S(1)}, bf16[512,512]{1,0:T(8,128)(2,1)}, u32[]{:S(2)}, u32[]{:S(2)}) collective-permute-start(bf16[512,512]{1,0:T(8,128)(2,1)S(1)} %convolution_convert_fusion), channel_id=1, source_target_pairs={{0,1},{1,2},{2,3},{3,0},{4,5},{5,6},{6,7},{7,4},{8,9},{9,10},{10,1... | collective-permute-start | bytes 1572872 | tf_op jit(solution)/shard_map/ppermute | solution.py:19
  220.3 14.6 %collective-permute-start.1 = (bf16[512,512]{1,0:T(8,128)(2,1)}, bf16[512,512]{1,0:T(8,128)(2,1)}, u32[]{:S(2)}, u32[]{:S(2)}) collective-permute-start(bf16[512,512]{1,0:T(8,128)(2,1)} %collective-permute-done), channel_id=1, source_target_pairs={{0,1},{1,2},{2,3},{3,0},{4,5},{5,6},{6,7},{7,4},{8,9},{9,10},{10,1... | collective-permute-start | bytes 1572872 | tf_op jit(solution)/shard_map/ppermute | solution.py:19
  235.0 13.9 %collective-permute-start.2 = (bf16[512,512]{1,0:T(8,128)(2,1)}, bf16[512,512]{1,0:T(8,128)(2,1)}, u32[]{:S(2)}, u32[]{:S(2)}) collective-permute-start(bf16[512,512]{1,0:T(8,128)(2,1)} %collective-permute-done.1), channel_id=1, source_target_pairs={{0,1},{1,2},{2,3},{3,0},{4,5},{5,6},{6,7},{7,4},{8,9},{9,10},{10,1... | collective-permute-start | bytes 1572872 | tf_op jit(solution)/shard_map/ppermute | solution.py:19
  237.7 186.8 %reduce-scatter.5.cloned.1.call-start = ((), (), s32[]{:S(2)}) async-start(), calls=%async_computation.4 | async-start | bytes 4718592 | tf_op jit(solution)/shard_map/reduce_scatter | solution.py:70
Sparse Core Ops, SparseCore 0:
  9.9 39.2 all-gather.1
  123.0 77.4 reduce-scatter.2
  237.8 132.7 all-reduce.1
  374.4 50.1 reduce-scatter.4
